TPU v7x, 32 devices: a whole 2x2x4 slice. The times are simulated.
32 devices in a mesh: dp: 8 (over z, x), ctx: 4 (over y, core).
Axes of the slice: x: 2, y: 2, z: 4, core: 2. Of those that a mesh axis runs over, the one named last changes fastest.
Arguments:
- inputs: bfloat16 [8, 512, 2048], P('dp', 'ctx'), may hold values from -8 to 8
- doc_ids: int32 [8, 512], P('dp', 'ctx'), may hold values from 0 to 3, never falling along the last dimension, each value on 1 to 256 neighbouring positions
- dilation: int32 [1], replicated, may hold values from 1 to 256
- filter_w: bfloat16 [2, 2048, 2048], P(None, 'dp', 'ctx'), may hold values from -0.09375 to 0.09375
- gate_w: bfloat16 [2, 2048, 2048], P(None, 'dp', 'ctx'), may hold values from -0.09375 to 0.09375
- filter_m: float32 [2, 2048, 2048], P(None, 'dp', 'ctx'), may hold values from -0.01171875 to 0.01171875
- filter_v: float32 [2, 2048, 2048], P(None, 'dp', 'ctx'), may hold values from 1e-07 to 4e-06
- gate_m: float32 [2, 2048, 2048], P(None, 'dp', 'ctx'), may hold values from -0.01171875 to 0.01171875
- gate_v: float32 [2, 2048, 2048], P(None, 'dp', 'ctx'), may hold values from 1e-07 to 4e-06
- cotangent: bfloat16 [8, 512, 2048], P('dp', 'ctx'), may hold values from -6 to 6
Outputs:
- layer_out: bfloat16 [8, 512, 2048], P('dp', 'ctx')
- input_grad: bfloat16 [8, 512, 2048], P('dp', 'ctx')
- new_filter_w: bfloat16 [2, 2048, 2048], P(None, 'dp', 'ctx')
- new_gate_w: bfloat16 [2, 2048, 2048], P(None, 'dp', 'ctx')
- new_filter_m: float32 [2, 2048, 2048], P(None, 'dp', 'ctx')
- new_filter_v: float32 [2, 2048, 2048], P(None, 'dp', 'ctx')
- new_gate_m: float32 [2, 2048, 2048], P(None, 'dp', 'ctx')
- new_gate_v: float32 [2, 2048, 2048], P(None, 'dp', 'ctx')
Inputs may be any that keep to these rules, and one draw needn't show every extreme that they name: `doc_ids`: document numbers never fall along a sequence; a document covers at most 256 positions.
All inputs are finite; a program needn't handle non-finite values.
Results may differ from a plain program's by a relative error of at most 0.0075.
Values may be sent and summed in bfloat16 or wider, within the bound.
No kernel may reach another device: no remote copies, remote signals or barrier semaphores. Data moves between devices by JAX's collectives and lax.ppermute only.
A program may use at most 128 MiB of HBM per device.

v0:
```python
import jax
import jax.numpy as jnp
from jax import lax
from jax.sharding import PartitionSpec as P

STEP = 10
BETA_ONE = 0.9
BETA_TWO = 0.95
LEARN_RATE = 0.001
EPSILON = 1e-08


def lagged_rows(sequence, seq_ids, shift_by):
    length = sequence.shape[0]
    start_row = length - shift_by
    padded = jnp.concatenate([jnp.zeros_like(sequence), sequence], axis=0)
    shifted = lax.dynamic_slice_in_dim(padded, start_row, length, 0)
    id_padded = jnp.concatenate([jnp.full((length,), -1, jnp.int32), seq_ids], axis=0)
    id_shifted = lax.dynamic_slice_in_dim(id_padded, start_row, length, 0)
    return jnp.where((id_shifted == seq_ids)[:, None], shifted, jnp.zeros_like(shifted))


def adam_update(weight, moment, second, gradient):
    new_moment = BETA_ONE * moment + (1.0 - BETA_ONE) * gradient
    new_second = BETA_TWO * second + (1.0 - BETA_TWO) * gradient * gradient
    first_fix = 1.0 - BETA_ONE**STEP
    second_fix = 1.0 - BETA_TWO**STEP
    step_size = new_moment / first_fix / (jnp.sqrt(new_second / second_fix) + EPSILON)
    new_weight = (weight.astype(jnp.float32) - LEARN_RATE * step_size).astype(jnp.bfloat16)
    return (new_weight, new_moment, new_second)


def per_device(
    inputs, doc_ids, dilation, filter_w, gate_w, filter_m, filter_v, gate_m, gate_v, cotangent
):
    gathered, gathered_ids = (
        lax.all_gather(inputs, "ctx", axis=1, tiled=True),
        lax.all_gather(doc_ids, "ctx", axis=1, tiled=True),
    )
    sequence = gathered[0]
    seq_ids = gathered_ids[0]
    shift_by = dilation[0]
    lagged = lagged_rows(sequence, seq_ids, shift_by)
    length = sequence.shape[0]
    columns = filter_w.shape[2]
    part_filter = lax.all_gather(filter_w, "dp", axis=1, tiled=True)
    part_gate = lax.all_gather(gate_w, "dp", axis=1, tiled=True)
    seq_cols = sequence
    lag_cols = lagged
    zero_part = jnp.concatenate([part_filter[0], part_gate[0]], axis=1)
    one_part = jnp.concatenate([part_filter[1], part_gate[1]], axis=1)
    pre_act = jnp.dot(seq_cols, zero_part, preferred_element_type=jnp.float32) + jnp.dot(
        lag_cols, one_part, preferred_element_type=jnp.float32
    )
    filter_tanh = jnp.tanh(pre_act[:, :columns])
    gate_sigmoid = jax.nn.sigmoid(pre_act[:, columns:])
    gated_cols = (filter_tanh * gate_sigmoid).astype(jnp.bfloat16)
    gated_rows = lax.all_to_all(gated_cols, "ctx", split_axis=0, concat_axis=1, tiled=True)
    layer_out = (inputs[0].astype(jnp.float32) + gated_rows.astype(jnp.float32)).astype(
        jnp.bfloat16
    )
    cot_cols = lax.all_to_all(cotangent[0], "ctx", split_axis=1, concat_axis=0, tiled=True)
    cot_float = cot_cols.astype(jnp.float32)
    filter_delta = (cot_float * gate_sigmoid * (1.0 - filter_tanh * filter_tanh)).astype(
        jnp.bfloat16
    )
    gate_delta = (cot_float * filter_tanh * gate_sigmoid * (1.0 - gate_sigmoid)).astype(
        jnp.bfloat16
    )
    pre_grad = jnp.concatenate([filter_delta, gate_delta], axis=1)
    back_filter, back_gate = (
        lax.all_gather(filter_w, "dp", axis=1, tiled=True),
        lax.all_gather(gate_w, "dp", axis=1, tiled=True),
    )
    back_zero = jnp.concatenate([back_filter[0], back_gate[0]], axis=1)
    back_one = jnp.concatenate([back_filter[1], back_gate[1]], axis=1)
    ahead_grad = jnp.concatenate([pre_grad, jnp.zeros_like(pre_grad)], axis=0)
    ahead_ids = jnp.concatenate([seq_ids, jnp.full((length,), -1, jnp.int32)], axis=0)
    row_count = cotangent.shape[1] * lax.axis_size("ctx")
    rows_ahead = lax.dynamic_slice_in_dim(ahead_grad, shift_by, row_count, 0)
    ids_later = lax.dynamic_slice_in_dim(ahead_ids, shift_by, row_count, 0)
    near_term = lax.dot_general(
        pre_grad, back_zero, (((1,), (1,)), ((), ())), preferred_element_type=jnp.float32
    )
    far_term = lax.dot_general(
        rows_ahead, back_one, (((1,), (1,)), ((), ())), preferred_element_type=jnp.float32
    )
    input_sum = lax.psum_scatter(
        (
            near_term
            + jnp.where((ids_later == seq_ids)[:, None], far_term, jnp.zeros_like(far_term))
        ).astype(jnp.bfloat16),
        "ctx",
        scatter_dimension=0,
        tiled=True,
    ).astype(jnp.float32)
    input_grad = (cotangent[0].astype(jnp.float32) + input_sum).astype(jnp.bfloat16)
    seq_cols = sequence
    lag_cols = lagged
    grad_zero = lax.dot_general(
        seq_cols, pre_grad, (((0,), (0,)), ((), ())), preferred_element_type=jnp.float32
    )
    grad_one = lax.dot_general(
        lag_cols, pre_grad, (((0,), (0,)), ((), ())), preferred_element_type=jnp.float32
    )
    summed = lax.psum_scatter(
        jnp.stack([grad_zero, grad_one], axis=1), "dp", scatter_dimension=0, tiled=True
    )
    tokens_all = length * lax.axis_size("dp")
    filter_grad = jnp.transpose(summed[:, :, :columns], (1, 0, 2)) / tokens_all
    gate_grad = jnp.transpose(summed[:, :, columns:], (1, 0, 2)) / tokens_all
    new_filter_w, new_filter_m, new_filter_v = adam_update(
        filter_w, filter_m, filter_v, filter_grad
    )
    new_gate_w, new_gate_m, new_gate_v = adam_update(gate_w, gate_m, gate_v, gate_grad)
    return (
        layer_out[None],
        input_grad[None],
        new_filter_w,
        new_gate_w,
        new_filter_m,
        new_filter_v,
        new_gate_m,
        new_gate_v,
    )


def solution(mesh):
    placed = (
        P("dp", "ctx", None),
        P("dp", "ctx"),
        P(),
        P(None, "dp", "ctx"),
        P(None, "dp", "ctx"),
        P(None, "dp", "ctx"),
        P(None, "dp", "ctx"),
        P(None, "dp", "ctx"),
        P(None, "dp", "ctx"),
        P("dp", "ctx", None),
    )
    return jax.shard_map(
        per_device,
        mesh=mesh,
        in_specs=placed,
        out_specs=(
            P("dp", "ctx", None),
            P("dp", "ctx", None),
            P(None, "dp", "ctx"),
            P(None, "dp", "ctx"),
            P(None, "dp", "ctx"),
            P(None, "dp", "ctx"),
            P(None, "dp", "ctx"),
            P(None, "dp", "ctx"),
        ),
        check_vma=False,
    )
```

profile of v0, /device:TPU:0, one launch (start us, length us, event | category | flops | bytes accessed | tf_op | source)
XLA Modules:
  0.0 541.8 jit_solution(2864115587601302465)
XLA Ops:
  7.2 0.0 all-gather.6.cloned.1.call-start
  7.2 0.7 all-gather.6.cloned.1.call-update
  7.9 0.0 copy-start.17
  7.9 0.0 all-gather.4.cloned.1.call-start
  8.0 0.7 all-gather.4.cloned.1.call-update
  8.7 0.0 all-gather.8.cloned.1.call-start
  8.7 0.7 all-gather.8.cloned.1.call-update
  9.4 1.4 all_to_all.22
  10.8 0.9 copy.19
  11.7 4.3 all-to-all-start.1
  16.0 0.0 reduce-scatter.3.cloned.1.call-start
  16.7 9.1 %all_gather.17 = s32[1,512]{1,0:T(1,128)S(1)} all-gather(s32[1,128]{1,0:T(1,128)S(1)} %copy-done.17), channel_id=1, replica_groups=mesh['dp'=8,'ctx'=4] {'ctx'}, dimensions={1}, use_global_device_ids=true | all-gather | bytes 2560 | tf_op jit(solution)/shard_map/all_gather | solution.py:38
  25.7 0.1 fusion.17
  25.8 59.9 %all-gather.6.cloned.1.call-done = bf16[2,2048,512]{2,1,0:T(8,128)(2,1)} async-done(((bf16[2,256,512]{2,1,0:T(8,128)(2,1)}), bf16[2,2048,512]{2,1,0:T(8,128)(2,1)}) %all-gather.6.cloned.1.call-update) | async-done | bytes 4194320 | tf_op jit(solution)/shard_map/all_gather | solution.py:47
  85.7 3.8 slice_bitcast_fusion.2
  89.5 69.7 %all-gather.4.cloned.1.call-done = bf16[2,2048,512]{2,1,0:T(8,128)(2,1)} async-done(((bf16[2,256,512]{2,1,0:T(8,128)(2,1)}), bf16[2,2048,512]{2,1,0:T(8,128)(2,1)}) %all-gather.4.cloned.1.call-update) | async-done | bytes 4194320 | tf_op jit(solution)/shard_map/all_gather | solution.py:46
  159.2 4.5 slice_bitcast_fusion.3
  163.7 18.2 %all-gather.8.cloned.1.call-done = bf16[1,512,2048]{2,1,0:T(8,128)(2,1)} async-done(((bf16[1,128,2048]{2,1,0:T(8,128)(2,1)}), bf16[1,512,2048]{2,1,0:T(8,128)(2,1)}) %all-gather.8.cloned.1.call-update) | async-done | bytes 2097168 | tf_op jit(solution)/shard_map/all_gather | solution.py:37
  181.9 4.6 fusion
  186.6 2.3 bitcast_add_fusion
  188.9 0.0 all-to-all-done.1
  188.9 0.0 copy-start.9
  188.9 0.0 copy-start.12
  188.9 1.4 fusion.9
  190.3 0.2 copy-done.9
  190.5 0.9 copy-done.12
  191.4 2.4 fusion.1
  193.8 0.0 copy-done.13
  193.8 0.0 copy-start.7
  193.8 0.1 pad_maximum_fusion.9
  193.9 1.4 copy-done.7
  195.4 3.8 add_convert_fusion
  199.2 0.0 reduce-scatter.3.cloned.1.call-update
  199.2 0.2 reduce-scatter.5.cloned.1.call-start
  199.4 0.8 copy-done.14
  200.2 2.6 convolution_bitcast_fusion
  202.8 2.4 convolution_bitcast_fusion.1
  205.2 6.2 %pad_maximum_fusion = f32[2048,2,1024]{0,2,1:T(8,128)} fusion(f32[2048,1,1024]{0,2,1:T(8,128)S(1)} %convolution_bitcast_fusion, f32[2048,1,1024]{0,2,1:T(8,128)S(1)} %convolution_bitcast_fusion.1), kind=kLoop, calls=%fused_computation | loop fusion | flops 4194304 | bytes 33554432 | tf_op jit(solution)/shard_map/stack | solution.py:107
  211.4 0.0 reduce-scatter.5.cloned.1.call-update
  211.4 0.0 copy-start.5
  211.4 0.0 copy-start.15
  211.4 4.5 all-to-all-start
  215.9 0.0 copy-start.16
  216.0 1.0 copy.24
  217.0 0.0 copy-done.5
  217.0 1.0 copy.20
  218.0 0.3 copy.25
  218.3 0.3 copy.26
  218.6 1.6 copy.23
  220.2 2.5 copy.21
  222.7 7.7 %all-to-all-done = bf16[4,128,512]{2,1,0:T(8,128)(2,1)} async-done(((bf16[4,128,512]{2,1,0:T(8,128)(2,1)}), bf16[4,128,512]{2,1,0:T(8,128)(2,1)}, u32[]{:S(2)}, u32[]{:S(2)}) %all-to-all-start) | async-done | bytes 524320 | tf_op jit(solution)/shard_map/all_to_all | solution.py:58
  230.5 1.2 convert_bitcast_fusion
  231.7 1.7 copy.18
  233.3 2.9 reshape.41
  236.2 2.3 add_convert_fusion.1
  238.5 2.1 fusion.13
  240.6 279.5 %reduce-scatter.5.cloned.1.call-done = f32[256,2,1024]{0,2,1:T(8,128)} async-done(((f32[2048,2,1024]{0,2,1:T(8,128)}), f32[256,2,1024]{0,2,1:T(8,128)}) %reduce-scatter.5.cloned.1.call-update) | async-done | bytes 2097168 | tf_op jit(solution)/shard_map/reduce_scatter | solution.py:106
  520.1 5.7 %subtract_convert_fusion = (bf16[2,256,512]{1,2,0:T(8,128)(2,1)}, f32[2,256,512]{1,2,0:T(8,128)}, f32[2,256,512]{1,2,0:T(8,128)}, bf16[2,256,512]{1,2,0:T(8,128)...) fusion(bf16[2,256,512]{1,2,0:T(8,128)(2,1)} %copy.24, f32[256,2,1024]{0,2,1:T(8,128)} %reduce-scatter.5.cloned.1.call-done, ...), kind=kLoop, calls=%fused_computation.37 | loop fusion | flops 8388608 | bytes 12582912 | tf_op jit(solution)/shard_map/convert_element_type | solution.py:29
  525.8 2.2 copy.27
  528.0 2.0 copy.28
  530.0 1.3 copy.29
  531.3 1.3 copy.30
  532.6 1.3 copy.31
  533.9 1.3 copy.32
  (28 shorter events, 0.1 us)
Async XLA Ops:
  7.2 78.5 %all-gather.6.cloned.1.call-start = ((), (), s32[]{:S(2)}) async-start(), calls=%async_computation.5 | async-start | bytes 4718592 | tf_op jit(solution)/shard_map/all_gather | solution.py:47
  7.9 8.7 %copy-start.17 = (s32[1,128]{1,0:T(1,128)S(1)}, s32[1,128]{1,0:T(1,128)}, u32[]{:S(2)}) copy-start(s32[1,128]{1,0:T(1,128)} %param.11) | copy-start | bytes 1540
  7.9 151.3 %all-gather.4.cloned.1.call-start = ((), (), s32[]{:S(2)}) async-start(), calls=%async_computation.4 | async-start | bytes 4718592 | tf_op jit(solution)/shard_map/all_gather | solution.py:46
  8.7 173.3 %all-gather.8.cloned.1.call-start = ((), (), s32[]{:S(2)}) async-start(), calls=%async_computation.6 | async-start | bytes 2621440 | tf_op jit(solution)/shard_map/all_gather | solution.py:37
  11.7 177.2 %all-to-all-start.1 = ((bf16[128,4,512]{2,0,1:T(8,128)(2,1)}), bf16[128,4,512]{2,0,1:T(8,128)(2,1)S(1)}, u32[]{:S(2)}, u32[]{:S(2)}) async-start(bf16[128,4,512]{2,0,1:T(8,128)(2,1)} %copy.19), calls=%async_computation.1 | async-start | bytes 1048576 | tf_op jit(solution)/shard_map/all_to_all | solution.py:62
  16.0 222.5 %reduce-scatter.3.cloned.1.call-start = ((), (), s32[]{:S(2)}) async-start(), calls=%async_computation.7 | async-start | bytes 2621440 | tf_op jit(solution)/shard_map/reduce_scatter | solution.py:88
  89.5 92.4 %copy-start.6 = (bf16[2048,512]{1,0:T(8,128)(2,1)}, bf16[2048,512]{1,0:T(8,128)(2,1)S(1)}, u32[]{:S(2)}) copy-start(bf16[2048,512]{1,0:T(8,128)(2,1)S(1)} %get-tuple-element.25) | copy-start | bytes 6291460
  181.9 4.6 copy-start.8
  181.9 4.6 copy-start.11
  181.9 4.6 copy-start.18
  188.9 1.6 copy-start.9
  188.9 2.5 copy-start.12
  190.3 3.4 copy-start.13
  191.4 2.5 copy-start.10
  193.8 1.6 copy-start.7
  195.4 4.1 copy-start.19
  199.2 1.0 copy-start.14
  199.2 320.9 %reduce-scatter.5.cloned.1.call-start = ((), (), s32[]{:S(2)}) async-start(), calls=%async_computation.8 | async-start | bytes 18874368 | tf_op jit(solution)/shard_map/reduce_scatter | solution.py:106
  211.4 4.6 copy-start.4
  211.4 5.6 %copy-start.5 = (bf16[2,256,512]{2,1,0:T(8,128)(2,1)S(1)}, bf16[2,256,512]{2,1,0:T(8,128)(2,1)}, u32[]{:S(2)}) copy-start(bf16[2,256,512]{2,1,0:T(8,128)(2,1)} %param.13) | copy-start | bytes 1572868
  211.4 6.6 %copy-start.15 = (f32[2,256,512]{2,1,0:T(8,128)S(1)}, f32[2,256,512]{2,1,0:T(8,128)}, u32[]{:S(2)}) copy-start(f32[2,256,512]{2,1,0:T(8,128)} %param.17) | copy-start | bytes 3145732
  211.4 19.1 %all-to-all-start = ((bf16[4,128,512]{2,1,0:T(8,128)(2,1)}), bf16[4,128,512]{2,1,0:T(8,128)(2,1)}, u32[]{:S(2)}, u32[]{:S(2)}) async-start(bf16[4,128,512]{2,1,0:T(8,128)(2,1)} %bitcast.8), calls=%async_computation | async-start | bytes 1048576 | tf_op jit(solution)/shard_map/all_to_all | solution.py:58
  215.9 2.4 copy-start.16
  525.8 4.2 copy-start.3
  525.8 5.6 %copy-start.2 = (f32[2,256,512]{1,2,0:T(8,128)S(1)}, f32[2,256,512]{1,2,0:T(8,128)}, u32[]{:S(2)}) copy-start(f32[2,256,512]{1,2,0:T(8,128)} %get-tuple-element.29) | copy-start | bytes 3145732
  530.0 2.6 copy-start.1
  531.3 2.6 copy-start
Sparse Core Ops, SparseCore 0:
  10.2 75.4 all-gather.5
  87.9 71.2 all-gather.3
  160.8 21.0 all-gather.7
  199.3 36.7 reduce-scatter.2
  239.8 280.2 reduce-scatter.4
where the time goes:
time: 542 us
  waiting for transfers between devices  437 us (81%)
  local copies, waits for them, and re-layouts  34.8 us (6%)
  other arithmetic  19 us (4%)
  matrix products  18.1 us (3%)
  between operations  14.7 us (3%)
  starting transfers between devices  9.11 us (2%)
  blocking collectives  9.06 us (2%)
    reduce_scatter x1, waiting for transfers between devices, per_device(): lax.psum_scatter(jnp.stack([grad_zero, grad_one], axis=1), 'dp', scatter_...  279 us
    all_gather x1, waiting for transfers between devices, per_device(): part_filter = lax.all_gather(filter_w, 'dp', axis=1, tiled=True)  69.7 us
    all_gather x1, waiting for transfers between devices, per_device(): part_gate = lax.all_gather(gate_w, 'dp', axis=1, tiled=True)  59.9 us
    unnamed x52, local copies, waits for them, and re-layouts  19.5 us
    all_gather x1, waiting for transfers between devices, per_device(): lax.all_gather(inputs, 'ctx', axis=1, tiled=True)  18.2 us
  transfers between devices with their start and end apart: 7, of which 5 were waited for; matrix products, arithmetic and copies ran while one was open for 8% of the time, Pallas kernels for 0%

commit v1 on v0

--- a/solution.py
+++ b/solution.py
@@ -43,8 +43,11 @@
     lagged = lagged_rows(sequence, seq_ids, shift_by)
     length = sequence.shape[0]
     columns = filter_w.shape[2]
-    part_filter = lax.all_gather(filter_w, "dp", axis=1, tiled=True)
-    part_gate = lax.all_gather(gate_w, "dp", axis=1, tiled=True)
+    part_filter, part_gate = jnp.split(
+        lax.all_gather(jnp.concatenate([filter_w, gate_w], axis=0), "dp", axis=1, tiled=True),
+        [filter_w.shape[0]],
+        axis=0,
+    )
     seq_cols = sequence
     lag_cols = lagged
     zero_part = jnp.concatenate([part_filter[0], part_gate[0]], axis=1)

time: 542 us -> 667 us (1.23)
  waiting for transfers between devices: 437 us -> 555 us
    all_gather x2 -> x3, waiting for transfers between devices: 130 us -> 249 us  [the longest x1 121 us: per_device(): lax.all_gather(jnp.concatenate([filter_w, gate_w], axis=0), 'dp', axis=1,...]
    squeeze x0 -> x2, local copies, waits for them, and re-layouts: none -> 8.93 us  [per_device(): back_zero = jnp.concatenate([back_filter[0], back_gate[0]], axis=1)]
  transfers between devices with their start and end apart: 7 -> 8, of which waited for: 5 -> 6; matrix products, arithmetic and copies ran while one was open for 8% -> 8% of each run, Pallas kernels for 0% -> 0%
where the time goes in v1:
time: 667 us
  waiting for transfers between devices  555 us (83%)
  local copies, waits for them, and re-layouts  39.3 us (6%)
  other arithmetic  21.2 us (3%)
  matrix products  18.1 us (3%)
  between operations  15 us (2%)
  starting transfers between devices  9.15 us (1%)
  blocking collectives  9.06 us (1%)
    reduce_scatter x1, waiting for transfers between devices, per_device(): lax.psum_scatter(jnp.stack([grad_zero, grad_one], axis=1), 'dp', scatter_...  279 us
    all_gather x1, waiting for transfers between devices, per_device(): lax.all_gather(jnp.concatenate([filter_w, gate_w], axis=0), 'dp', axis=1,...  121 us
    all_gather x1, waiting for transfers between devices, per_device(): lax.all_gather(filter_w, 'dp', axis=1, tiled=True)  69 us
    all_gather x1, waiting for transfers between devices, per_device(): lax.all_gather(gate_w, 'dp', axis=1, tiled=True)  58.8 us
    unnamed x52, local copies, waits for them, and re-layouts  18.8 us
    all_gather x1, waiting for transfers between devices, per_device(): lax.all_gather(inputs, 'ctx', axis=1, tiled=True)  16.4 us
  transfers between devices with their start and end apart: 8, of which 6 were waited for; matrix products, arithmetic and copies ran while one was open for 8% of the time, Pallas kernels for 0%

profile of v1, /device:TPU:0, one launch (start us, length us, event | category | flops | bytes accessed | tf_op | source)
XLA Modules:
  0.0 666.6 jit_solution(1630367566443953525)
XLA Ops:
  7.2 0.0 all-gather.11.cloned.1.call-start
  7.2 0.7 all-gather.11.cloned.1.call-update
  7.9 0.0 copy-start.6
  7.9 0.0 all-gather.9.cloned.1.call-start
  8.0 0.7 all-gather.9.cloned.1.call-update
  8.7 0.0 all-gather.5.cloned.1.call-start
  8.7 2.3 pad_maximum_fusion.1
  11.0 0.0 all-gather.5.cloned.1.call-update
  11.0 0.0 copy-start.17
  11.0 0.0 all-gather.7.cloned.1.call-start
  11.1 0.5 all-gather.7.cloned.1.call-update
  11.6 0.4 all_to_all.22
  12.0 0.9 copy.19
  12.9 4.3 all-to-all-start.1
  17.8 9.1 %all_gather.17 = s32[1,512]{1,0:T(1,128)S(1)} all-gather(s32[1,128]{1,0:T(1,128)S(1)} %copy-done.17), channel_id=1, replica_groups=mesh['dp'=8,'ctx'=4] {'ctx'}, dimensions={1}, use_global_device_ids=true | all-gather | bytes 2560 | tf_op jit(solution)/shard_map/all_gather | solution.py:38
  26.9 0.1 fusion.34
  26.9 58.8 %all-gather.11.cloned.1.call-done = bf16[2,2048,512]{2,1,0:T(8,128)(2,1)} async-done(((bf16[2,256,512]{2,1,0:T(8,128)(2,1)}), bf16[2,2048,512]{2,1,0:T(8,128)(2,1)}) %all-gather.11.cloned.1.call-update) | async-done | bytes 4194320 | tf_op jit(solution)/shard_map/all_gather | solution.py:76
  85.7 4.5 slice_bitcast_fusion.2
  90.2 69.0 %all-gather.9.cloned.1.call-done = bf16[2,2048,512]{2,1,0:T(8,128)(2,1)} async-done(((bf16[2,256,512]{2,1,0:T(8,128)(2,1)}), bf16[2,2048,512]{2,1,0:T(8,128)(2,1)}) %all-gather.9.cloned.1.call-update) | async-done | bytes 4194320 | tf_op jit(solution)/shard_map/all_gather | solution.py:75
  159.2 4.4 slice_bitcast_fusion.3
  163.7 121.4 %all-gather.5.cloned.1.call-done = bf16[4,2048,512]{2,1,0:T(8,128)(2,1)} async-done(((bf16[4,256,512]{2,1,0:T(8,128)(2,1)}), bf16[4,2048,512]{2,1,0:T(8,128)(2,1)}) %all-gather.5.cloned.1.call-update) | async-done | bytes 8388624 | tf_op jit(solution)/shard_map/all_gather | solution.py:47
  285.0 5.8 slice_bitcast_fusion.7
  290.8 16.4 %all-gather.7.cloned.1.call-done = bf16[1,512,2048]{2,1,0:T(8,128)(2,1)} async-done(((bf16[1,128,2048]{2,1,0:T(8,128)(2,1)}), bf16[1,512,2048]{2,1,0:T(8,128)(2,1)}) %all-gather.7.cloned.1.call-update) | async-done | bytes 2097168 | tf_op jit(solution)/shard_map/all_gather | solution.py:37
  307.2 4.6 fusion.4
  311.9 2.3 bitcast_add_fusion
  314.2 0.0 all-to-all-done.1
  314.2 1.4 fusion.26
  315.6 0.1 pad_maximum_fusion.2
  315.7 0.1 copy-done.10
  315.8 1.6 copy-done.8
  317.4 2.5 fusion.12
  320.0 3.8 add_convert_fusion
  323.7 0.0 reduce-scatter.3.cloned.1.call-update
  323.8 0.2 reduce-scatter.5.cloned.1.call-start
  324.0 0.8 copy-done.12
  324.8 2.6 convolution_bitcast_fusion
  327.4 2.4 convolution_bitcast_fusion.1
  329.7 6.2 pad_maximum_fusion
  335.9 0.0 reduce-scatter.5.cloned.1.call-update
  335.9 0.0 copy-start.1
  335.9 0.0 copy-start.15
  336.0 4.5 all-to-all-start
  340.5 0.0 copy-start.16
  340.5 1.0 copy.24
  341.5 1.0 copy.20
  342.5 0.0 copy-done.15
  342.5 0.3 copy.25
  342.8 0.3 copy.26
  343.2 1.6 copy.23
  344.8 2.5 copy.21
  347.3 7.7 %all-to-all-done = bf16[4,128,512]{2,1,0:T(8,128)(2,1)} async-done(((bf16[4,128,512]{2,1,0:T(8,128)(2,1)}), bf16[4,128,512]{2,1,0:T(8,128)(2,1)}, u32[]{:S(2)}, u32[]{:S(2)}) %all-to-all-start) | async-done | bytes 524320 | tf_op jit(solution)/shard_map/all_to_all | solution.py:61
  355.0 1.2 convert_bitcast_fusion
  356.2 1.7 copy.18
  357.8 2.9 reshape.41
  360.8 2.3 add_convert_fusion.1
  363.0 2.1 fusion.30
  365.2 279.4 %reduce-scatter.5.cloned.1.call-done = f32[256,2,1024]{0,2,1:T(8,128)} async-done(((f32[2048,2,1024]{0,2,1:T(8,128)}), f32[256,2,1024]{0,2,1:T(8,128)}) %reduce-scatter.5.cloned.1.call-update) | async-done | bytes 2097168 | tf_op jit(solution)/shard_map/reduce_scatter | solution.py:109
  644.6 5.7 subtract_convert_fusion
  650.3 2.2 copy.27
  652.4 2.0 copy.28
  654.5 1.3 copy.29
  655.8 1.3 copy.30
  657.1 1.3 copy.31
  658.4 1.3 copy.32
  (33 shorter events, 0.1 us)
Async XLA Ops:
  7.2 78.5 %all-gather.11.cloned.1.call-start = ((), (), s32[]{:S(2)}) async-start(), calls=%async_computation.7 | async-start | bytes 4718592 | tf_op jit(solution)/shard_map/all_gather | solution.py:76
  7.9 3.7 copy-start.6
  7.9 151.3 %all-gather.9.cloned.1.call-start = ((), (), s32[]{:S(2)}) async-start(), calls=%async_computation.6 | async-start | bytes 4718592 | tf_op jit(solution)/shard_map/all_gather | solution.py:75
  8.7 276.4 %all-gather.5.cloned.1.call-start = ((), (), s32[]{:S(2)}) async-start(), calls=%async_computation.4 | async-start | bytes 9437184 | tf_op jit(solution)/shard_map/all_gather | solution.py:47
  11.0 6.8 %copy-start.17 = (s32[1,128]{1,0:T(1,128)S(1)}, s32[1,128]{1,0:T(1,128)}, u32[]{:S(2)}) copy-start(s32[1,128]{1,0:T(1,128)} %param.11) | copy-start | bytes 1540
  11.0 296.2 %all-gather.7.cloned.1.call-start = ((), (), s32[]{:S(2)}) async-start(), calls=%async_computation.5 | async-start | bytes 2621440 | tf_op jit(solution)/shard_map/all_gather | solution.py:37
  12.9 301.3 %all-to-all-start.1 = ((bf16[128,4,512]{2,0,1:T(8,128)(2,1)}), bf16[128,4,512]{2,0,1:T(8,128)(2,1)S(1)}, u32[]{:S(2)}, u32[]{:S(2)}) async-start(bf16[128,4,512]{2,0,1:T(8,128)(2,1)} %copy.19), calls=%async_computation.1 | async-start | bytes 1048576 | tf_op jit(solution)/shard_map/all_to_all | solution.py:65
  17.1 345.9 %reduce-scatter.3.cloned.1.call-start = ((), (), s32[]{:S(2)}) async-start(), calls=%async_computation.8 | async-start | bytes 2621440 | tf_op jit(solution)/shard_map/reduce_scatter | solution.py:91
  307.2 4.6 copy-start.13
  307.2 4.6 copy-start.14
  307.2 4.6 copy-start.18
  314.2 1.6 copy-start.10
  315.6 4.3 copy-start.11
  315.6 1.8 copy-start.8
  317.4 2.5 copy-start.7
  317.4 2.5 copy-start.9
  319.9 4.0 copy-start.19
  323.7 1.0 copy-start.12
  323.8 320.8 %reduce-scatter.5.cloned.1.call-start = ((), (), s32[]{:S(2)}) async-start(), calls=%async_computation.9 | async-start | bytes 18874368 | tf_op jit(solution)/shard_map/reduce_scatter | solution.py:109
  335.9 4.6 copy-start
  335.9 5.6 copy-start.1
  335.9 6.6 copy-start.15
  336.0 19.1 %all-to-all-start = ((bf16[4,128,512]{2,1,0:T(8,128)(2,1)}), bf16[4,128,512]{2,1,0:T(8,128)(2,1)}, u32[]{:S(2)}, u32[]{:S(2)}) async-start(bf16[4,128,512]{2,1,0:T(8,128)(2,1)} %bitcast.8), calls=%async_computation | async-start | bytes 1048576 | tf_op jit(solution)/shard_map/all_to_all | solution.py:61
  340.5 2.4 copy-start.16
  650.2 4.2 copy-start.5
  650.2 5.6 copy-start.4
  654.5 2.6 copy-start.3
  655.8 2.6 copy-start.2
Sparse Core Ops, SparseCore 0:
  10.2 75.5 all-gather.10
  87.9 71.2 all-gather.8
  162.0 122.9 all-gather.4
  286.4 20.7 all-gather.6
  323.9 36.7 reduce-scatter.2
  364.3 280.2 reduce-scatter.4
